TPU v7x, 512 devices: a whole 4x4x16 slice. The times are simulated.
512 devices in a mesh: call: 64 (over z, y_hi, core), tensor: 8 (over x, y_lo).
Axes of the slice: x: 4, y: 4 (y_hi: 2, y_lo: 2; y = y_hi * 2 + y_lo), z: 16, core: 2. Of those that a mesh axis runs over, the one named last changes fastest.
Arguments:
- queries: bfloat16 [64, 768, 8192], P('call', None, 'tensor'), may hold values from -8 to 8
- child_kv: bfloat16 [64, 2, 768, 1024], P('call', None, None, 'tensor'), may hold values from -6 to 6
- summ_kv: bfloat16 [64, 2, 256, 1024], P('call', None, None, 'tensor'), may hold values from -6 to 6
- instr_pool: bfloat16 [64, 1024, 2, 1024], P('call', 'tensor'), may hold values from -16 to 16
- child_len: int32 [64], P('call'), may hold values from 256 to 768, as said below
- summ_len: int32 [64], P('call'), may hold values from 64 to 256, as said below
- owner_group: int32 [1], replicated, may hold values from 0 to 63
Outputs:
- attended: bfloat16 [64, 768, 8192], P('call', None, 'tensor')
Inputs may be any that keep to these rules, and one draw needn't show every extreme that they name: `child_len`: one call has exactly 768 child tokens and one exactly 256. `summ_len`: one call has exactly 256 summary tokens and one exactly 64.
All inputs are finite; a program needn't handle non-finite values.
Results may differ from a plain program's by a relative error of at most 0.006.
Values may be sent and summed in bfloat16 or wider, within the bound.
A program may use at most 64 MiB of HBM per device.

v0:
```python
import math
import jax
import jax.numpy as jnp
from jax import lax
from jax.sharding import PartitionSpec as P

HD = 128
NEG = -1e30


def broadcast(value, axis, source):
    kept = jnp.where(lax.axis_index(axis) == source, value, 0).astype(value.dtype)
    return lax.psum(kept, axis)


def passed_along(block, axis, distance):
    devices = range(lax.axis_size(axis))
    route = [(i - distance, i) for i in devices if i - distance in devices]
    return lax.ppermute(block, axis, route)


def head_split(packed, heads):
    total = packed.shape[0]
    width = packed.shape[1]
    return packed.reshape(total, heads, width // heads).transpose(1, 0, 2)


def partial_softmax(query_head, key_rows, value_rows, allowed):
    score_scale = 1.0 / math.sqrt(query_head.shape[1])
    scores = (
        lax.dot_general(
            query_head, key_rows, (((1,), (1,)), ((), ())), preferred_element_type=jnp.float32
        )
        * score_scale
    )
    scores = jnp.where(allowed, scores, NEG)
    maxima = jnp.max(scores, axis=1, keepdims=True)
    expons = jnp.where(allowed, jnp.exp(scores - maxima), 0.0)
    totals = jnp.sum(expons, axis=1, keepdims=True)
    weights = expons.astype(jnp.bfloat16)
    return (maxima, totals, jnp.dot(weights, value_rows, preferred_element_type=jnp.float32))


def over_heads(query_heads, key_heads, value_heads, allowed):
    group = query_heads.shape[0] // key_heads.shape[0]

    def single(pair):
        query_head, number = pair
        key_rows = lax.dynamic_index_in_dim(key_heads, number // group, 0, keepdims=False)
        value_rows = lax.dynamic_index_in_dim(value_heads, number // group, 0, keepdims=False)
        return partial_softmax(query_head, key_rows, value_rows, allowed)

    return lax.map(single, (query_heads, jnp.arange(query_heads.shape[0], dtype=jnp.int32)))


def shards(queries, child_kv, summ_kv, instr_pool, child_len, summ_len, owner_group):
    query_mat = queries[0]
    length = query_mat.shape[0]
    heads = query_mat.shape[1] // HD
    kv_heads = child_kv.shape[3] // HD
    fetched = broadcast(instr_pool, "call", owner_group[0])
    instr_local = lax.all_to_all(fetched, "tensor", split_axis=3, concat_axis=1, tiled=True)
    sibling_kv, sibling_len = passed_along((summ_kv, summ_len), "call", 1)
    instr_count = instr_local.shape[1]
    summ_count = summ_kv.shape[2]
    positions = jnp.arange(length, dtype=jnp.int32)
    own_allowed = positions[None, :] <= positions[:, None]
    remote_allowed = jnp.concatenate(
        [
            jnp.ones((length, instr_count), bool),
            jnp.broadcast_to(
                jnp.arange(summ_count, dtype=jnp.int32)[None, :] < sibling_len[0],
                (length, summ_count),
            ),
        ],
        1,
    )
    remote_keys = jnp.concatenate([instr_local[0, :, 0], sibling_kv[0, 0]], 0)
    remote_values = jnp.concatenate([instr_local[0, :, 1], sibling_kv[0, 1]], 0)
    query_heads = head_split(query_mat, heads)
    key_all = jnp.concatenate([remote_keys, child_kv[0, 0]], 0)
    value_all = jnp.concatenate([remote_values, child_kv[0, 1]], 0)
    allowed = jnp.concatenate([remote_allowed, own_allowed], 1)
    maxima, totals, sums = over_heads(
        query_heads, head_split(key_all, kv_heads), head_split(value_all, kv_heads), allowed
    )
    combined = sums / totals
    result = combined.transpose(1, 0, 2).reshape(length, heads * HD)
    result = jnp.where((positions < child_len[0])[:, None], result, 0.0)
    return result.astype(jnp.bfloat16)[None]


def solution(mesh):
    in_specs = (
        P("call", None, "tensor"),
        P("call", None, None, "tensor"),
        P("call", None, None, "tensor"),
        P("call", "tensor", None, None),
        P("call"),
        P("call"),
        P(),
    )
    out_specs = P("call", None, "tensor")
    return jax.shard_map(shards, mesh=mesh, in_specs=in_specs, out_specs=out_specs, check_vma=False)
```

profile of v0, /device:TPU:8, one launch (start us, length us, event | category | flops | bytes accessed | tf_op | source)
XLA Modules:
  0.0 634.9 jit_solution(1127240871721148693)
XLA Ops:
  6.5 2.8 copy.22
  10.0 1.2 broadcast_select_fusion
  11.2 1.7 collective-permute-start
  13.0 5.0 collective-permute-start.1
  18.0 0.2 iota_compare_fusion
  18.2 2.6 copy.21
  21.5 0.6 iota_compare_fusion.2
  22.1 525.9 %all-reduce.2.cloned.1.call-done = bf16[1,128,2,1024]{1,2,0,3:T(2,128)(2,1)} async-done(((bf16[1,128,2,1024]{1,2,0,3:T(2,128)(2,1)}), bf16[1,128,2,1024]{1,2,0,3:T(2,128)(2,1)}) %all-reduce.2.cloned.1.call-update) | async-done | bytes 524304 | tf_op jit(solution)/shard_map/psum | solution.py:13
  548.0 5.7 all-to-all-start
  553.7 0.6 pad_add_fusion
  554.3 8.1 %all-to-all-done = bf16[1,128,2,1024]{1,2,0,3:T(2,128)(2,1)S(1)} async-done(((bf16[1,128,2,1024]{1,2,0,3:T(2,128)(2,1)}), bf16[1,128,2,1024]{1,2,0,3:T(2,128)(2,1)S(1)}, u32[]{:S(2)}, u32[]{:S(2)}) %all-to-all-start) | async-done | bytes 524320 | tf_op jit(solution)/shard_map/all_to_all | solution.py:62
  562.4 0.5 copy.23
  563.0 59.4 %while.13 = (s32[]{:T(128)}, f32[8,768,1]{1,0,2:T(8,128)S(1)}, f32[8,768,128]{2,1,0:T(8,128)}, bf16[8,768,128]{1,2,0:T(8,128)(2,1)}, bf16[1,2048,128]{2,1,0:T(8,...) while((s32[]{:T(128)}, f32[8,768,1]{1,0,2:T(8,128)S(1)}, ...), condition=%wide.region_4.5_spmd, body=%wide.region_1.4_spmd.sunk | while | flops 825752064 | bytes 25257056 | solution.py:53
  563.0 2.5 fusion.27
  565.5 2.5 fusion.29
  568.0 2.3 fusion.28
  570.3 0.1 dynamic_update_slice.14
  570.4 2.5 fusion.27
  572.9 2.5 fusion.29
  575.4 2.3 fusion.28
  577.7 0.1 dynamic_update_slice.14
  577.8 2.5 fusion.27
  580.3 2.5 fusion.29
  582.8 2.3 fusion.28
  585.1 0.1 dynamic_update_slice.14
  585.3 2.5 fusion.27
  587.7 2.5 fusion.29
  590.3 2.3 fusion.28
  592.6 0.1 dynamic_update_slice.14
  592.7 2.5 fusion.27
  595.2 2.5 fusion.29
  597.7 2.3 fusion.28
  600.0 0.1 dynamic_update_slice.14
  600.1 2.5 fusion.27
  602.6 2.5 fusion.29
  605.1 2.3 fusion.28
  607.5 0.1 dynamic_update_slice.14
  607.6 2.5 fusion.27
  610.1 2.5 fusion.29
  612.6 2.3 fusion.28
  615.0 2.5 fusion.27
  617.5 2.5 fusion.29
  620.0 2.3 fusion.28
  622.3 0.1 dynamic_update_slice.14
  622.4 2.4 divide_bitcast_fusion
  624.8 1.0 copy.25
  625.9 0.7 reshape.46
  626.6 1.5 select_convert_fusion
  (24 shorter events, 0.3 us)
Async XLA Ops:
  6.5 541.5 %all-reduce.2.cloned.1.call-start = ((), (), s32[]{:S(2)}) async-start(), calls=%async_computation.1 | async-start | bytes 1048576 | tf_op jit(solution)/shard_map/psum | solution.py:13
  6.5 14.9 %copy-start = (bf16[1,2,768,128]{3,2,1,0:T(8,128)(2,1)S(1)}, bf16[1,2,768,128]{3,2,1,0:T(8,128)(2,1)}, u32[]{:S(2)}) copy-start(bf16[1,2,768,128]{3,2,1,0:T(8,128)(2,1)} %param.10) | copy-start | bytes 1179652
  11.2 543.0 %collective-permute-start = (bf16[1,2,256,128]{3,2,1,0:T(8,128)(2,1)}, bf16[1,2,256,128]{3,2,1,0:T(8,128)(2,1)S(1)}, u32[]{:S(2)}, u32[]{:S(2)}) collective-permute-start(bf16[1,2,256,128]{3,2,1,0:T(8,128)(2,1)} %param.11), channel_id=1, source_target_pairs={{0,8},{8,16},{16,24},{24,32},{32,40},{40,48},{48,56},{56,64},{64,7... | collective-permute-start | bytes 393224 | tf_op jit(solution)/shard_map/ppermute | solution.py:19
  13.0 8.5 %collective-permute-start.1 = (s32[1]{0:T(128)}, s32[1]{0:T(128)}, u32[]{:S(2)}, u32[]{:S(2)}) collective-permute-start(s32[1]{0:T(128)} %param.14), channel_id=1, source_target_pairs={{0,8},{8,16},{16,24},{24,32},{32,40},{40,48},{48,56},{56,64},{64,7... | collective-permute-start | bytes 20 | tf_op jit(solution)/shard_map/ppermute | solution.py:19
  548.0 14.4 %all-to-all-start = ((bf16[1,128,2,1024]{1,2,0,3:T(2,128)(2,1)}), bf16[1,128,2,1024]{1,2,0,3:T(2,128)(2,1)S(1)}, u32[]{:S(2)}, u32[]{:S(2)}) async-start(bf16[1,128,2,1024]{1,2,0,3:T(2,128)(2,1)} %all-reduce.2.cloned.1.call-done), calls=%async_computation | async-start | bytes 1048576 | tf_op jit(solution)/shard_map/all_to_all | solution.py:62
Sparse Core Ops, SparseCore 0:
  11.4 536.5 all-reduce.1
where the time goes:
time: 635 us
  waiting for transfers between devices  534 us (84%)
  matrix products  40.1 us (6%)
  other arithmetic  24.9 us (4%)
  between operations  14.8 us (2%)
  starting transfers between devices  12.5 us (2%)
  local copies, waits for them, and re-layouts  8.4 us (1%)
    psum x1, waiting for transfers between devices, broadcast(): return lax.psum(kept, axis)  526 us
    dot_general x8, matrix products, partial_softmax(): jnp.dot(weights, value_rows, preferred_element_type=jnp.float32)  20.2 us
    dot_general x8, matrix products, partial_softmax(): lax.dot_general(query_head, key_rows, (((1,), (1,)), ((), ())), preferred...  19.9 us
    reduce_sum x8, other arithmetic, partial_softmax(): totals = jnp.sum(expons, axis=1, keepdims=True)  18.4 us
  transfers between devices with their start and end apart: 4, of which 2 were waited for; matrix products, arithmetic and copies ran while one was open for 1% of the time, Pallas kernels for 0%

commit v1 on v0

--- a/solution.py
+++ b/solution.py
@@ -10,7 +10,7 @@
 
 def broadcast(value, axis, source):
     kept = jnp.where(lax.axis_index(axis) == source, value, 0).astype(value.dtype)
-    return lax.psum(kept, axis)
+    return jnp.sum(lax.all_gather(kept, axis), axis=0)
 
 
 def passed_along(block, axis, distance):

time: 635 us -> 387 us (0.61)
  the two profiles are of different devices: /device:TPU:8 before, /device:TPU:1 now
where the time goes in v1:
time: 387 us
  waiting for transfers between devices  274 us (71%)
  matrix products  40.1 us (10%)
  other arithmetic  37.2 us (10%)
  between operations  14.9 us (4%)
  starting transfers between devices  12.1 us (3%)
  local copies, waits for them, and re-layouts  7.9 us (2%)
    all_gather x1, waiting for transfers between devices, broadcast(): return jnp.sum(lax.all_gather(kept, axis), axis=0)  266 us
    dot_general x8, matrix products, partial_softmax(): jnp.dot(weights, value_rows, preferred_element_type=jnp.float32)  20.2 us
    dot_general x8, matrix products, partial_softmax(): lax.dot_general(query_head, key_rows, (((1,), (1,)), ((), ())), preferred...  19.9 us
    reduce_sum x8, other arithmetic, partial_softmax(): totals = jnp.sum(expons, axis=1, keepdims=True)  18.4 us
    reduce_sum x1, other arithmetic, broadcast(): return jnp.sum(lax.all_gather(kept, axis), axis=0)  11.4 us
    all_to_all x1, waiting for transfers between devices, shards(): lax.all_to_all(fetched, 'tensor', split_axis=3, concat_axis=1, tiled=True)  8.57 us
    ppermute x2, starting transfers between devices, passed_along(): return lax.ppermute(block, axis, route)  8.13 us
  transfers between devices with their start and end apart: 4, of which 2 were waited for; matrix products, arithmetic and copies ran while one was open for 5% of the time, Pallas kernels for 0%

profile of v1, /device:TPU:1, one launch (start us, length us, event | category | flops | bytes accessed | tf_op | source)
XLA Modules:
  0.0 386.7 jit_solution(10874893331683096867)
XLA Ops:
  7.2 2.1 copy_select_fusion
  9.3 6.2 %collective-permute-start = (bf16[1,2,256,128]{3,2,1,0:T(8,128)(2,1)}, bf16[1,2,256,128]{3,2,1,0:T(8,128)(2,1)S(1)}, u32[]{:S(2)}, u32[]{:S(2)}) collective-permute-start(bf16[1,2,256,128]{3,2,1,0:T(8,128)(2,1)} %param.11), channel_id=1, source_target_pairs={{0,8},{8,16},{16,24},{24,32},{32,40},{40,48},{48,56},{56,64},{64,7... | collective-permute-start | bytes 393224 | tf_op jit(solution)/shard_map/ppermute | solution.py:19
  15.5 1.9 collective-permute-start.1
  17.5 2.6 copy.16
  20.7 0.2 iota_compare_fusion
  21.0 0.6 iota_compare_fusion.2
  21.6 265.6 %all-gather.3.cloned.1.call-done = bf16[64,128,2,1024]{3,1,2,0:T(8,128)(2,1)} async-done(((bf16[1,128,2,1024]{3,1,2,0:T(8,128)(2,1)}), bf16[64,128,2,1024]{3,1,2,0:T(8,128)(2,1)}) %all-gather.3.cloned.1.call-update) | async-done | bytes 33554448 | tf_op jit(solution)/shard_map/all_gather | solution.py:13
  287.2 11.4 %reduce.2 = bf16[128,2,1024]{2,0,1:T(8,128)(2,1)S(1)} reduce(bf16[64,128,2,1024]{3,1,2,0:T(8,128)(2,1)} %all-gather.3.cloned.1.call-done, bf16[]{:T(256)} %constant.58.clone.1), dimensions={0}, to_apply=%region_0.1 | reduce | flops 16515072 | bytes 34078720 | tf_op jit(solution)/shard_map/reduce_sum | solution.py:13
  298.6 0.5 copy.31
  299.2 1.9 copy.19
  301.0 4.0 %all-to-all-start = ((bf16[1,128,2,1024]{1,2,0,3:T(2,128)(2,1)}), bf16[1,128,2,1024]{1,2,0,3:T(2,128)(2,1)S(1)}, u32[]{:S(2)}, u32[]{:S(2)}) async-start(bf16[1,128,2,1024]{1,2,0,3:T(2,128)(2,1)} %copy.19), calls=%async_computation | async-start | bytes 1048576 | tf_op jit(solution)/shard_map/all_to_all | solution.py:62
  305.0 0.6 pad_add_fusion
  305.6 8.6 %all-to-all-done = bf16[1,128,2,1024]{1,2,0,3:T(2,128)(2,1)S(1)} async-done(((bf16[1,128,2,1024]{1,2,0,3:T(2,128)(2,1)}), bf16[1,128,2,1024]{1,2,0,3:T(2,128)(2,1)S(1)}, u32[]{:S(2)}, u32[]{:S(2)}) %all-to-all-start) | async-done | bytes 524320 | tf_op jit(solution)/shard_map/all_to_all | solution.py:62
  314.3 0.3 copy.21
  314.7 59.5 %while.13 = (s32[]{:T(128)}, f32[8,768,1]{1,0,2:T(8,128)S(1)}, f32[8,768,128]{2,1,0:T(8,128)}, bf16[8,768,128]{1,2,0:T(8,128)(2,1)}, bf16[1,2048,128]{2,1,0:T(8,...) while((s32[]{:T(128)}, f32[8,768,1]{1,0,2:T(8,128)S(1)}, ...), condition=%wide.region_4.5_spmd, body=%wide.region_1.4_spmd.sunk | while | flops 825752064 | bytes 25257056 | solution.py:53
  314.7 2.5 fusion.27
  317.2 2.5 fusion.29
  319.7 2.3 fusion.28
  322.0 0.1 dynamic_update_slice.14
  322.1 2.5 fusion.27
  324.6 2.5 fusion.29
  327.1 2.3 fusion.28
  329.4 0.1 dynamic_update_slice.14
  329.5 2.5 fusion.27
  332.0 2.5 fusion.29
  334.6 2.3 fusion.28
  336.9 0.1 dynamic_update_slice.14
  337.0 2.5 fusion.27
  339.5 2.5 fusion.29
  342.0 2.3 fusion.28
  344.4 2.5 fusion.27
  346.9 2.5 fusion.29
  349.4 2.3 fusion.28
  351.7 0.1 dynamic_update_slice.14
  351.8 2.5 fusion.27
  354.3 2.5 fusion.29
  356.8 2.3 fusion.28
  359.3 2.5 fusion.27
  361.7 2.6 fusion.29
  364.3 2.3 fusion.28
  366.6 0.1 dynamic_update_slice.14
  366.7 2.5 fusion.27
  369.2 2.5 fusion.29
  371.7 2.3 fusion.28
  374.1 2.4 divide_bitcast_fusion
  376.6 1.0 copy.23
  377.6 0.7 reshape.47
  378.3 1.5 select_convert_fusion
  (27 shorter events, 0.6 us)
Async XLA Ops:
  6.5 14.4 %copy-start = (bf16[1,2,768,128]{3,2,1,0:T(8,128)(2,1)S(1)}, bf16[1,2,768,128]{3,2,1,0:T(8,128)(2,1)}, u32[]{:S(2)}) copy-start(bf16[1,2,768,128]{3,2,1,0:T(8,128)(2,1)} %param.10) | copy-start | bytes 1179652
  6.5 280.7 %all-gather.3.cloned.1.call-start = ((), (), s32[]{:S(2)}) async-start(), calls=%async_computation.1 | async-start | bytes 34078720 | tf_op jit(solution)/shard_map/all_gather | solution.py:13
  9.3 296.3 %collective-permute-start = (bf16[1,2,256,128]{3,2,1,0:T(8,128)(2,1)}, bf16[1,2,256,128]{3,2,1,0:T(8,128)(2,1)S(1)}, u32[]{:S(2)}, u32[]{:S(2)}) collective-permute-start(bf16[1,2,256,128]{3,2,1,0:T(8,128)(2,1)} %param.11), channel_id=1, source_target_pairs={{0,8},{8,16},{16,24},{24,32},{32,40},{40,48},{48,56},{56,64},{64,7... | collective-permute-start | bytes 393224 | tf_op jit(solution)/shard_map/ppermute | solution.py:19
  15.5 5.4 %collective-permute-start.1 = (s32[1]{0:T(128)}, s32[1]{0:T(128)}, u32[]{:S(2)}, u32[]{:S(2)}) collective-permute-start(s32[1]{0:T(128)} %param.14), channel_id=1, source_target_pairs={{0,8},{8,16},{16,24},{24,32},{32,40},{40,48},{48,56},{56,64},{64,7... | collective-permute-start | bytes 20 | tf_op jit(solution)/shard_map/ppermute | solution.py:19
  301.0 13.1 %all-to-all-start = ((bf16[1,128,2,1024]{1,2,0,3:T(2,128)(2,1)}), bf16[1,128,2,1024]{1,2,0,3:T(2,128)(2,1)S(1)}, u32[]{:S(2)}, u32[]{:S(2)}) async-start(bf16[1,128,2,1024]{1,2,0,3:T(2,128)(2,1)} %copy.19), calls=%async_computation | async-start | bytes 1048576 | tf_op jit(solution)/shard_map/all_to_all | solution.py:62
Sparse Core Ops, SparseCore 0:
  10.6 276.5 all-gather.2
